TPU v7x, 32 devices: a whole 2x2x4 slice. The times are simulated.
32 devices in a mesh: slab: 16 (over z, y, core), tile: 2 (over x).
Axes of the slice: x: 2, y: 2, z: 4, core: 2. Of those that a mesh axis runs over, the one named last changes fastest.
Arguments:
- positions: float32 [64, 3, 128], P(('slab', 'tile')), may hold values from 0 to 150
- weights: float32 [64, 128], P(('slab', 'tile')), may hold values from -6 to 6
- counts: int32 [64], P(('slab', 'tile')), may hold values from 64 to 128
- pairs: int32 [32, 8, 2], P(('slab', 'tile')), may hold values from 0 to 7, as said below
- pair_count: int32 [32], P(('slab', 'tile')), may hold values from 1 to 8
Outputs:
- harmonics: float32 [64, 360, 128], P(('slab', 'tile'))
- zeta: float32 [64, 6, 100], P(('slab', 'tile'))
Inputs may be any that keep to these rules, and one draw needn't show every extreme that they name: pairs[d, p, 0] is below 2. pairs[d, p, 1] = h * 2 * 2 + t2 * 2 + k2 names block k2 of tile t2 in the device's slab (h = 0) or in the slab below it (h = 1, never on the first slab); with h = 0 the named block is never earlier in the slab's order of blocks than the local one. Among the first pair_count entries of all devices, each unordered pair of blocks appears at most once; a block paired with itself is allowed.
All inputs are finite; a program needn't handle non-finite values.
Results may differ from a plain program's by a relative error of at most 0.0003.
Values sent between devices are 32-bit elements; how exact they have to be, the bound alone decides.
No kernel may reach another device: no remote copies, remote signals or barrier semaphores. Data moves between devices by JAX's collectives and lax.ppermute only.
A program may use at most 64 MiB of HBM per device.

v0:
```python
import math

import jax
import jax.numpy as jnp
import numpy as np
from jax import lax
from jax.experimental import pallas as pl
from jax.experimental.pallas import tpu as pltpu
from jax.sharding import PartitionSpec as P

NBIN = 10
DEGREES = 6
NHARM = DEGREES * DEGREES
BPAD = 16
SPACING = 150.0 / (NBIN + 1)
SUB = 8
LANES = 128
COLS = (NBIN + 1) * SUB
GROUPS = LANES // SUB
HROWS = NHARM * SUB
OCTETS = -(-NHARM // SUB)
BOTH = ("slab", "tile")
f32 = jnp.float32
bf16 = jnp.bfloat16


def seat_of(l, m):
    return l * l + l + m


def legendre_sums():
    out = []
    for l in range(DEGREES):
        series = np.polynomial.legendre.leg2poly([0.0] * l + [1.0])
        for signed in range(-l, l + 1):
            m = abs(signed)
            norm = math.sqrt((2 * l + 1) / (4 * math.pi) * math.factorial(l - m) / math.factorial(l + m))
            if m > 0:
                norm *= math.sqrt(2.0)
            poly = np.polynomial.polynomial.polyder(series, m) if m else series
            out.append([(seat_of(m + a, signed), norm * float(c)) for a, c in enumerate(poly) if abs(c) > 1e-9])
    return out


def products_of(x, y, z, w):
    cosine, sine = [w], [None]
    for m in range(1, DEGREES):
        if m == 1:
            cosine.append(w * x)
            sine.append(w * y)
        else:
            cosine.append(cosine[-1] * x - sine[-1] * y)
            sine.append(sine[-1] * x + cosine[-2] * y)
    out = [None] * NHARM
    for m in range(DEGREES):
        for sign in (1, -1) if m else (1,):
            term = cosine[m] if sign > 0 else sine[m]
            for l in range(m, DEGREES):
                out[seat_of(l, sign * m)] = term
                if l < DEGREES - 1:
                    term = term * z
    return out


def halves(v):
    high = v.astype(bf16)
    return high, (v - high.astype(f32)).astype(bf16)


def stacked_halves(values):
    pairs = [halves(jnp.concatenate(values[k : k + 2], axis=0)) for k in range(0, len(values), 2)]
    return [jnp.concatenate(part, axis=0) for part in zip(*pairs)]


def operands(own, row):
    ex, ey, ez = (row[r] - own[r] for r in range(3))
    r2 = ex * ex + ey * ey + ez * ez
    rs = lax.rsqrt(jnp.maximum(r2, 1e-30))
    tau = r2 * rs
    inv = jnp.minimum(rs, SPACING)
    gaps = [jnp.minimum(jnp.abs(tau - (b + 1.0)), 1.0) for b in range(NBIN)]
    w = jnp.broadcast_to(row[3], (SUB, LANES))
    return stacked_halves(products_of(ex * inv, ey * inv, ez * inv, w)) + stacked_halves(gaps)


def pack_kernel(base, lists, pos, weights, pairs, counts, pair_count, out):
    nblk = weights.shape[0]
    out[...] = jnp.zeros_like(out)
    out[base : base + 2, 0:lists] = pairs[0].astype(f32)
    lane = lax.broadcasted_iota(jnp.int32, (1, LANES), 1)
    numbers = counts[...].astype(f32)
    line = jnp.where(lane == 0, jnp.broadcast_to(pair_count[...].astype(f32), (1, LANES)), 0.0)
    for k in range(nblk):
        count = jnp.broadcast_to(numbers[:, k : k + 1], (1, LANES))
        line = jnp.where(lane == k + 1, count, line)
        for r in range(3):
            out[r * nblk + k : r * nblk + k + 1, :] = pos[r, k : k + 1, :]
        out[3 * nblk + k : 3 * nblk + k + 1, :] = weights[k : k + 1, :] * (lane.astype(f32) < count).astype(f32)
    out[base + 2 : base + 3, :] = line


def kernel(tiles, nblk, rows_dev, base, lists, *refs):
    (own_in, one_in, two_in, harm, zeta, meta, sems, data, chunks, tally, wide, acc, low, grams) = refs
    sources = (own_in, one_in, two_in)
    span = tiles * nblk
    me = lax.axis_index("tile")
    parity = lax.rem(lax.axis_index("slab"), 2)
    below = 2 - parity

    def seat(t):
        return jnp.bitwise_xor(t, me) if tiles == 2 else t

    copies = []
    for a, src in enumerate(sources):
        for t in range(tiles):
            n = len(copies)
            lines = src.at[pl.ds(t * rows_dev + base, 3), :]
            copies.append(pltpu.make_async_copy(lines, meta.at[pl.ds(3 * n, 3), :], sems.at[n]))
    for c in copies:
        c.start()
    for k in range(nblk):
        tally[k] = 0
    scale = jnp.where(lax.broadcasted_iota(jnp.int32, (4, LANES), 0) < 3, 1.0 / SPACING, 1.0)
    for a in range(3):
        for t in range(tiles):
            for k in range(nblk):
                rows = sources[a][pl.ds(t * rows_dev + k, 4, stride=nblk), :]
                data[(a * tiles + t) * nblk + k, 0:4, :] = rows * scale
    for k in range(nblk):
        turned = data[seat(me) * nblk + k].T
        for r in range(3):
            wide[k, r] = jnp.broadcast_to(turned[:, r : r + 1], (LANES, LANES))
    for c in copies:
        c.wait()
    lane = lax.broadcasted_iota(jnp.int32, (SUB, LANES), 1)

    def number(line, which, at):
        return meta[3 * line + which, at].astype(jnp.int32)

    def length(line):
        return number(line, 2, 0)

    def add_edge(mine, a, t, blk):
        line = a * tiles + seat(t)
        n = tally[mine]
        c, r = lax.shift_right_logical(n, 7), lax.bitwise_and(n, LANES - 1)
        turned = pltpu.roll(data[line * nblk + blk], r, axis=1)
        chunks[mine, c] = jnp.where(lane >= r, turned, chunks[mine, c])
        chunks[mine, c + 1] = jnp.where(lane < r, turned, 0.0)
        tally[mine] = n + number(line, 2, 1 + blk)

    def entry(line, p):
        b = number(line, 1, p)
        h = lax.div(b, span)
        rem = b - h * span
        t2 = lax.div(rem, nblk)
        return number(line, 0, p), h, t2, rem - t2 * nblk

    own_line = seat(me)

    def own_list(p, c):
        a, h, t2, k2 = entry(own_line, p)
        add_edge(a, h * below, t2, k2)

        @pl.when((h == 0) & (t2 == me) & (k2 != a))
        def _():
            add_edge(k2, 0, me, a)

        return c

    lax.fori_loop(0, length(own_line), own_list, 0)

    def neighbour(i, c):
        half = lax.div(i, tiles)
        t = i - half * tiles
        a = half * (1 + parity)
        line = a * tiles + seat(t)

        def body(p, c2):
            k, h, t2, k2 = entry(line, p)

            @pl.when((h == half) & (t2 == me))
            def _():
                add_edge(k2, a, t, k)

            return c2

        @pl.when((half == 1) | (t != me))
        def _():
            lax.fori_loop(0, length(line), body, 0)

        return c

    lax.fori_loop(0, 2 * tiles, neighbour, 0)

    lane_block = lax.shift_right_logical(lane, 3)
    point_of = lax.bitwise_and(lane, SUB - 1)
    sums = legendre_sums()
    swaps, wanted = [], set(range(NBIN + 1))
    for bit in (1, 2, 4, 8):
        swaps.insert(0, (bit, sorted(wanted)))
        wanted |= {x ^ bit for x in wanted}

    def block(mine, carry):
        home = seat(me) * nblk + mine

        def add_chunks(first, count, fresh=False):
            rows = [[chunks[mine, first + q, r : r + 1, :] for r in range(4)] for q in range(count)]
            ones = jnp.ones((SUB, LANES), f32)
            blank = jnp.concatenate([ones, jnp.zeros((LANES - COLS, LANES), f32)], axis=0).astype(bf16)
            zero = jnp.zeros((NBIN * SUB, LANES), bf16)
            last = jnp.zeros((2 * SUB, LANES), bf16)
            for g in range(GROUPS):
                own = [wide[mine, r, g * SUB : (g + 1) * SUB, :] for r in range(3)]
                left, right = [], []
                for q in range(count):
                    yh, yl, rh, rl = operands(own, rows[q])
                    left += [yh, yl]
                    right += [jnp.concatenate([rh, blank, rl, last], axis=0), jnp.concatenate([rh, blank, zero, last], axis=0)]
                d = lax.dot_general(
                    jnp.concatenate(left, axis=1),
                    jnp.concatenate(right, axis=1),
                    (((1,), (1,)), ((), ())),
                    preferred_element_type=f32,
                )
                d = d[:, 0:COLS] + d[:, LANES : LANES + COLS]
                acc[g, 0:HROWS, 0:COLS] = d if fresh else acc[g, 0:HROWS, 0:COLS] + d

        n_chunks = lax.div(tally[mine] + (LANES - 1), LANES)

        @pl.when(n_chunks < 2)
        def _():
            acc[...] = jnp.zeros_like(acc)

        @pl.when(n_chunks >= 2)
        def _():
            add_chunks(0, 2, fresh=True)

        start = jnp.where(n_chunks < 2, 0, 2)
        fours = lax.shift_right_logical(n_chunks - start, 2)

        def four(i, c):
            add_chunks(start + 4 * i, 4)
            return c

        lax.fori_loop(0, fours, four, 0)
        left_over = n_chunks - start - 4 * fours
        for count in range(1, 4):

            @pl.when(left_over == count)
            def _():
                add_chunks(n_chunks - count, count)

        w = data[home, 3:4, :]
        plain, next_l = [], 0
        for octet in range(OCTETS):
            got = min(SUB, NHARM - octet * SUB)
            cur = []
            for g in range(GROUPS):
                out = None
                for i in range(SUB):
                    v = acc[g, pl.ds(octet * SUB * SUB + i, got, stride=SUB), :]
                    out = v if i == 0 else jnp.where(point_of[:got] == i, v, out)
                if got < SUB:
                    out = jnp.concatenate([out, jnp.zeros((SUB - got, LANES), f32)], axis=0)
                cur.append(out)
            for bit, wanted in swaps:
                new = [None] * GROUPS
                for x in wanted:
                    if x & bit:
                        other = pltpu.roll(cur[x ^ bit], LANES - bit * SUB, axis=1)
                    else:
                        other = pltpu.roll(cur[x ^ bit], bit * SUB, axis=1)
                    new[x] = jnp.where(lax.bitwise_and(lane_block, bit) == (x & bit), cur[x], other)
                cur = new
            for b in range(NBIN):
                low[pl.ds(octet * SUB * NBIN + b, SUB, stride=NBIN), :] = cur[NBIN] - cur[b]
            for k in range(octet * SUB, octet * SUB + got):
                plain.append(low[k * NBIN : (k + 1) * NBIN, :])
            while next_l < DEGREES and (next_l + 1) * (next_l + 1) <= len(plain):
                left, right = [], []
                for k in range(next_l * next_l, (next_l + 1) * (next_l + 1)):
                    h = sum(plain[k2] * c for k2, c in sums[k])
                    harm[mine, k * NBIN : (k + 1) * NBIN, :] = h
                    h = jnp.concatenate([h, jnp.zeros((BPAD - NBIN, LANES), f32)], axis=0)
                    bh, bl = halves(h)
                    ah, al = halves(h * w)
                    left += [ah, al, ah]
                    right += [bh, bh, bl]
                grams[mine, next_l] = lax.dot_general(
                    jnp.concatenate(left, axis=1),
                    jnp.concatenate(right, axis=1),
                    (((1,), (1,)), ((), ())),
                    preferred_element_type=f32,
                )
                next_l += 1
        return carry

    lax.fori_loop(0, nblk, block, 0)

    col = lax.broadcasted_iota(jnp.int32, (BPAD, LANES), 1)
    row = lax.broadcasted_iota(jnp.int32, (BPAD, LANES), 0)
    flat_col = (lax.rem(col, NBIN) == row).astype(f32).astype(bf16)
    flat_row = lax.div(col, NBIN) == row
    both = halves(grams[...].reshape(nblk * DEGREES * BPAD, BPAD) * (1.0 / LANES))
    line = jnp.dot(
        jnp.concatenate(both, axis=1), jnp.concatenate([flat_col, flat_col], axis=0), preferred_element_type=f32
    )
    for mine in range(nblk):
        for l in range(DEGREES):
            at = (mine * DEGREES + l) * BPAD
            flat = jnp.sum(jnp.where(flat_row, line[at : at + BPAD], 0.0), axis=0, keepdims=True)
            zeta[l, mine : mine + 1, :] = flat[:, : NBIN * NBIN]


def shards(positions, weights, counts, pairs, pair_count):
    nblk, _, points = positions.shape
    lists = pairs.shape[1]
    tiles = lax.axis_size("tile")
    slabs = lax.axis_size("slab")
    base = -(-nblk * 4 // SUB) * SUB
    rows_dev = base + SUB
    vmem = pl.BlockSpec(memory_space=pltpu.VMEM)
    packed = pl.pallas_call(
        lambda *refs: pack_kernel(base, lists, *refs),
        out_shape=jax.ShapeDtypeStruct((rows_dev, points), f32),
        in_specs=[vmem] * 5,
        out_specs=vmem,
        compiler_params=pltpu.CompilerParams(vmem_limit_bytes=1024 * 1024),
    )(positions.transpose(1, 0, 2), weights, pairs.transpose(0, 2, 1), counts[None], pair_count[None])

    def move(value, hop):
        route = []
        for s in range(slabs):
            for t in range(tiles):
                s2, t2 = hop(s, t)
                if 0 <= s2 < slabs:
                    route.append((s * tiles + t, s2 * tiles + t2))
        return lax.ppermute(value, BOTH, route)

    if tiles == 2:
        slab = jnp.concatenate([packed, move(packed, lambda s, t: (s, 1 - t))], axis=0)
    else:
        slab = lax.all_gather(packed, "tile", axis=0, tiled=True)
    near = move(slab, lambda s, t: (s + 1 - 2 * (s % 2), t))
    far = move(slab, lambda s, t: (s - 1 + 2 * (s % 2), t))

    deepest = lists * (2 * tiles + 1) + 2
    body = lambda *refs: kernel(tiles, nblk, rows_dev, base, lists, *refs)
    harm, zeta = pl.pallas_call(
        body,
        out_shape=(
            jax.ShapeDtypeStruct((nblk, NHARM * NBIN, points), f32),
            jax.ShapeDtypeStruct((DEGREES, nblk, NBIN * NBIN), f32),
        ),
        in_specs=[vmem] * 3,
        out_specs=(vmem, vmem),
        scratch_shapes=[
            pltpu.SMEM((9 * tiles, points), f32),
            pltpu.SemaphoreType.DMA((3 * tiles,)),
            pltpu.VMEM((3 * tiles * nblk, SUB, points), f32),
            pltpu.VMEM((nblk, deepest, SUB, points), f32),
            pltpu.SMEM((nblk,), jnp.int32),
            pltpu.VMEM((nblk, 3, points, points), f32),
            pltpu.VMEM((GROUPS, OCTETS * SUB * SUB, LANES), f32),
            pltpu.VMEM((OCTETS * SUB * NBIN, points), f32),
            pltpu.VMEM((nblk, DEGREES, BPAD, BPAD), f32),
        ],
        compiler_params=pltpu.CompilerParams(vmem_limit_bytes=24 * 1024 * 1024),
    )(slab, near, far)
    return harm, zeta.transpose(1, 0, 2)


def solution(mesh):
    return jax.shard_map(
        shards,
        mesh=mesh,
        in_specs=(
            P(("slab", "tile"), None, None),
            P(("slab", "tile"), None),
            P(("slab", "tile")),
            P(("slab", "tile"), None, None),
            P(("slab", "tile")),
        ),
        out_specs=(P(("slab", "tile"), None, None), P(("slab", "tile"), None, None)),
        check_vma=False,
    )
```

profile of v0, /device:TPU:1, one launch (start us, length us, event | category | flops | bytes accessed | tf_op | source)
XLA Modules:
  0.0 22.1 jit_solution(9047434625260135921)
XLA Ops:
  1.3 0.0 copy-start
  1.3 0.0 copy-start.2
  1.3 0.0 copy-start.1
  1.3 0.0 copy-start.3
  1.3 0.6 %copy-done = f32[2,3,128]{2,0,1:T(2,128)S(1)} copy-done((f32[2,3,128]{2,0,1:T(2,128)S(1)}, f32[2,3,128]{2,0,1:T(2,128)}, u32[]{:S(2)}) %copy-start) | copy-done | bytes 3096
  2.0 0.0 copy-done.2
  2.0 0.0 copy-done.1
  2.0 0.0 copy-done.3
  2.0 0.1 shard_map.68
  2.1 2.0 %collective-permute-start = (f32[16,128]{1,0:T(8,128)S(1)}, f32[16,128]{1,0:T(8,128)S(1)}, u32[]{:S(2)}, u32[]{:S(2)}) collective-permute-start(f32[16,128]{1,0:T(8,128)S(1)} %shard_map.68), channel_id=1, source_target_pairs={{0,1},{1,0},{2,3},{3,2},{4,5},{5,4},{6,7},{7,6},{8,9},{9,8},{10,11... | collective-permute-start | bytes 24584 | tf_op jit(solution)/shard_map/ppermute | solution.py:339
  4.1 1.0 %collective-permute-done = f32[16,128]{1,0:T(8,128)S(1)} collective-permute-done((f32[16,128]{1,0:T(8,128)S(1)}, f32[16,128]{1,0:T(8,128)S(1)}, u32[]{:S(2)}, u32[]{:S(2)}) %collective-permute-start) | collective-permute-done | bytes 8224 | tf_op jit(solution)/shard_map/ppermute | solution.py:339
  5.1 5.1 %collective-permute-start.2 = (f32[32,128]{1,0:T(8,128)S(1)}, f32[32,128]{1,0:T(8,128)S(1)}, u32[]{:S(2)}, u32[]{:S(2)}) collective-permute-start(f32[32,128]{1,0:T(8,128)S(1)} %pad_maximum_fusion.refs_0_), channel_id=1, source_target_pairs={{2,4},{3,5},{4,2},{5,3},{6,8},{7,9},{8,6},{9,7},{10,12},{11,13},{1... | collective-permute-start | bytes 49160 | tf_op jit(solution)/shard_map/ppermute | solution.py:339
  10.3 0.1 collective-permute-start.1
  10.3 1.3 %collective-permute-done.2.refs_2_ = f32[32,128]{1,0:T(8,128)S(1)} collective-permute-done((f32[32,128]{1,0:T(8,128)S(1)}, f32[32,128]{1,0:T(8,128)S(1)}, u32[]{:S(2)}, u32[]{:S(2)}) %collective-permute-start.2) | collective-permute-done | bytes 16416 | tf_op jit(solution)/shard_map/ppermute | solution.py:339
  11.7 0.0 collective-permute-done.1.refs_1_
  11.7 10.4 %shard_map.69 = (f32[2,360,128]{2,1,0:T(8,128)}, f32[6,2,100]{2,1,0:T(2,128)}) custom-call(f32[32,128]{1,0:T(8,128)S(1)} %pad_maximum_fusion.refs_0_, f32[32,128]{1,0:T(8,128)S(1)} %collective-permute-done.1.refs_1_, f32[32,128]{1,0:T(8,128)S(1)} %collective-permute-done.2.refs_2_), custom_call_target="tpu_custom_call" | custom-call | tf_op jit(solution)/shard_map/pallas_call | solution.py:350
  (1 shorter events, 0.0 us)
Async XLA Ops:
  1.3 0.7 %copy-start = (f32[2,3,128]{2,0,1:T(2,128)S(1)}, f32[2,3,128]{2,0,1:T(2,128)}, u32[]{:S(2)}) copy-start(f32[2,3,128]{2,0,1:T(2,128)} %param.5) | copy-start | bytes 9220
  1.3 0.7 %copy-start.2 = (s32[1,8,2]{1,2,0:T(2,128)S(1)}, s32[1,8,2]{1,2,0:T(2,128)}, u32[]{:S(2)}) copy-start(s32[1,8,2]{1,2,0:T(2,128)} %param.8) | copy-start | bytes 196
  1.3 0.7 %copy-start.1 = (f32[2,128]{1,0:T(2,128)S(1)}, f32[2,128]{1,0:T(2,128)}, u32[]{:S(2)}) copy-start(f32[2,128]{1,0:T(2,128)} %refs_1_.1) | copy-start | bytes 3076
  1.3 0.7 %copy-start.3 = (s32[2]{0:T(128)S(1)}, s32[2]{0:T(128)}, u32[]{:S(2)}) copy-start(s32[2]{0:T(128)} %param.7) | copy-start | bytes 28
  2.1 3.1 %collective-permute-start = (f32[16,128]{1,0:T(8,128)S(1)}, f32[16,128]{1,0:T(8,128)S(1)}, u32[]{:S(2)}, u32[]{:S(2)}) collective-permute-start(f32[16,128]{1,0:T(8,128)S(1)} %shard_map.68), channel_id=1, source_target_pairs={{0,1},{1,0},{2,3},{3,2},{4,5},{5,4},{6,7},{7,6},{8,9},{9,8},{10,11... | collective-permute-start | bytes 24584 | tf_op jit(solution)/shard_map/ppermute | solution.py:339
  5.1 6.5 %collective-permute-start.2 = (f32[32,128]{1,0:T(8,128)S(1)}, f32[32,128]{1,0:T(8,128)S(1)}, u32[]{:S(2)}, u32[]{:S(2)}) collective-permute-start(f32[32,128]{1,0:T(8,128)S(1)} %pad_maximum_fusion.refs_0_), channel_id=1, source_target_pairs={{2,4},{3,5},{4,2},{5,3},{6,8},{7,9},{8,6},{9,7},{10,12},{11,13},{1... | collective-permute-start | bytes 49160 | tf_op jit(solution)/shard_map/ppermute | solution.py:339
  10.3 1.4 %collective-permute-start.1 = (f32[32,128]{1,0:T(8,128)S(1)}, f32[32,128]{1,0:T(8,128)S(1)}, u32[]{:S(2)}, u32[]{:S(2)}) collective-permute-start(f32[32,128]{1,0:T(8,128)S(1)} %pad_maximum_fusion.refs_0_), channel_id=1, source_target_pairs={{0,2},{1,3},{2,0},{3,1},{4,6},{5,7},{6,4},{7,5},{8,10},{9,11},{10,... | collective-permute-start | bytes 49160 | tf_op jit(solution)/shard_map/ppermute | solution.py:339
where the time goes:
time: 22.3 us; the launch traced here: 22.1 us
  Pallas kernels  10.5 us (47%)
  starting transfers between devices  7.2 us (32%)
  waiting for transfers between devices  2.37 us (11%)
  between operations  1.33 us (6%)
  local copies, waits for them, and re-layouts  0.68 us (3%)
    pallas_call x1, Pallas kernels, shards(): pl.pallas_call(body, out_shape=(jax.ShapeDtypeStruct((nblk, NHARM * NBIN,...  10.4 us
    ppermute x3, starting transfers between devices, move(): return lax.ppermute(value, BOTH, route)  7.2 us
    ppermute x3, waiting for transfers between devices, move(): return lax.ppermute(value, BOTH, route)  2.37 us
    unnamed x8, local copies, waits for them, and re-layouts  0.68 us
  transfers between devices with their start and end apart: 3, of which 2 were waited for; matrix products, arithmetic and copies ran while one was open for 0% of the time, Pallas kernels for 0%

commit v1 on v0

--- a/solution.py
+++ b/solution.py
@@ -228,24 +228,27 @@
 
         n_chunks = lax.div(tally[mine] + (LANES - 1), LANES)
 
-        @pl.when(n_chunks < 2)
+        lead = jnp.where(n_chunks <= 4, n_chunks, jnp.where(lax.bitwise_and(n_chunks, 3) == 1, 2, 4))
+
+        @pl.when(lead == 0)
         def _():
             acc[...] = jnp.zeros_like(acc)
 
-        @pl.when(n_chunks >= 2)
-        def _():
-            add_chunks(0, 2, fresh=True)
-
-        start = jnp.where(n_chunks < 2, 0, 2)
-        fours = lax.shift_right_logical(n_chunks - start, 2)
+        for count in range(1, 5):
+
+            @pl.when(lead == count)
+            def _():
+                add_chunks(0, count, fresh=True)
+
+        fours = lax.shift_right_logical(n_chunks - lead, 2)
 
         def four(i, c):
-            add_chunks(start + 4 * i, 4)
+            add_chunks(lead + 4 * i, 4)
             return c
 
         lax.fori_loop(0, fours, four, 0)
-        left_over = n_chunks - start - 4 * fours
-        for count in range(1, 4):
+        left_over = n_chunks - lead - 4 * fours
+        for count in (2, 3):
 
             @pl.when(left_over == count)
             def _():

time: 22.3 us -> 21 us (0.942)
  Pallas kernels: 10.5 us -> 9.02 us
    pallas_call x1, Pallas kernels: 10.4 us -> 8.95 us  [shards(): pl.pallas_call(body, out_shape=(jax.ShapeDtypeStruct((nblk, NHARM * NBIN,...]
where the time goes in v1:
time: 21 us; the launch traced here: 20.6 us
  Pallas kernels  9.02 us (43%)
  starting transfers between devices  7.2 us (34%)
  waiting for transfers between devices  2.37 us (11%)
  between operations  1.33 us (6%)
  local copies, waits for them, and re-layouts  0.68 us (3%)
    pallas_call x1, Pallas kernels, shards(): pl.pallas_call(body, out_shape=(jax.ShapeDtypeStruct((nblk, NHARM * NBIN,...  8.95 us
    ppermute x3, starting transfers between devices, move(): return lax.ppermute(value, BOTH, route)  7.2 us
    ppermute x3, waiting for transfers between devices, move(): return lax.ppermute(value, BOTH, route)  2.37 us
    unnamed x8, local copies, waits for them, and re-layouts  0.68 us
  transfers between devices with their start and end apart: 3, of which 2 were waited for; matrix products, arithmetic and copies ran while one was open for 0% of the time, Pallas kernels for 0%

profile of v1, /device:TPU:1, one launch (start us, length us, event | category | flops | bytes accessed | tf_op | source)
XLA Modules:
  0.0 20.6 jit_solution(3133667603599792622)
XLA Ops:
  1.3 0.0 copy-start
  1.3 0.0 copy-start.2
  1.3 0.0 copy-start.1
  1.3 0.0 copy-start.3
  1.3 0.6 %copy-done = f32[2,3,128]{2,0,1:T(2,128)S(1)} copy-done((f32[2,3,128]{2,0,1:T(2,128)S(1)}, f32[2,3,128]{2,0,1:T(2,128)}, u32[]{:S(2)}) %copy-start) | copy-done | bytes 3096
  2.0 0.0 copy-done.2
  2.0 0.0 copy-done.1
  2.0 0.0 copy-done.3
  2.0 0.1 shard_map.68
  2.1 2.0 %collective-permute-start = (f32[16,128]{1,0:T(8,128)S(1)}, f32[16,128]{1,0:T(8,128)S(1)}, u32[]{:S(2)}, u32[]{:S(2)}) collective-permute-start(f32[16,128]{1,0:T(8,128)S(1)} %shard_map.68), channel_id=1, source_target_pairs={{0,1},{1,0},{2,3},{3,2},{4,5},{5,4},{6,7},{7,6},{8,9},{9,8},{10,11... | collective-permute-start | bytes 24584 | tf_op jit(solution)/shard_map/ppermute | solution.py:342
  4.1 1.0 %collective-permute-done = f32[16,128]{1,0:T(8,128)S(1)} collective-permute-done((f32[16,128]{1,0:T(8,128)S(1)}, f32[16,128]{1,0:T(8,128)S(1)}, u32[]{:S(2)}, u32[]{:S(2)}) %collective-permute-start) | collective-permute-done | bytes 8224 | tf_op jit(solution)/shard_map/ppermute | solution.py:342
  5.1 5.1 %collective-permute-start.2 = (f32[32,128]{1,0:T(8,128)S(1)}, f32[32,128]{1,0:T(8,128)S(1)}, u32[]{:S(2)}, u32[]{:S(2)}) collective-permute-start(f32[32,128]{1,0:T(8,128)S(1)} %pad_maximum_fusion.refs_0_), channel_id=1, source_target_pairs={{2,4},{3,5},{4,2},{5,3},{6,8},{7,9},{8,6},{9,7},{10,12},{11,13},{1... | collective-permute-start | bytes 49160 | tf_op jit(solution)/shard_map/ppermute | solution.py:342
  10.3 0.1 collective-permute-start.1
  10.3 1.3 %collective-permute-done.2.refs_2_ = f32[32,128]{1,0:T(8,128)S(1)} collective-permute-done((f32[32,128]{1,0:T(8,128)S(1)}, f32[32,128]{1,0:T(8,128)S(1)}, u32[]{:S(2)}, u32[]{:S(2)}) %collective-permute-start.2) | collective-permute-done | bytes 16416 | tf_op jit(solution)/shard_map/ppermute | solution.py:342
  11.7 0.0 collective-permute-done.1.refs_1_
  11.7 8.9 %shard_map.69 = (f32[2,360,128]{2,1,0:T(8,128)}, f32[6,2,100]{2,1,0:T(2,128)}) custom-call(f32[32,128]{1,0:T(8,128)S(1)} %pad_maximum_fusion.refs_0_, f32[32,128]{1,0:T(8,128)S(1)} %collective-permute-done.1.refs_1_, f32[32,128]{1,0:T(8,128)S(1)} %collective-permute-done.2.refs_2_), custom_call_target="tpu_custom_call" | custom-call | tf_op jit(solution)/shard_map/pallas_call | solution.py:353
  (1 shorter events, 0.0 us)
Async XLA Ops:
  1.3 0.7 %copy-start = (f32[2,3,128]{2,0,1:T(2,128)S(1)}, f32[2,3,128]{2,0,1:T(2,128)}, u32[]{:S(2)}) copy-start(f32[2,3,128]{2,0,1:T(2,128)} %param.5) | copy-start | bytes 9220
  1.3 0.7 %copy-start.2 = (s32[1,8,2]{1,2,0:T(2,128)S(1)}, s32[1,8,2]{1,2,0:T(2,128)}, u32[]{:S(2)}) copy-start(s32[1,8,2]{1,2,0:T(2,128)} %param.8) | copy-start | bytes 196
  1.3 0.7 %copy-start.1 = (f32[2,128]{1,0:T(2,128)S(1)}, f32[2,128]{1,0:T(2,128)}, u32[]{:S(2)}) copy-start(f32[2,128]{1,0:T(2,128)} %refs_1_.1) | copy-start | bytes 3076
  1.3 0.7 %copy-start.3 = (s32[2]{0:T(128)S(1)}, s32[2]{0:T(128)}, u32[]{:S(2)}) copy-start(s32[2]{0:T(128)} %param.7) | copy-start | bytes 28
  2.1 3.1 %collective-permute-start = (f32[16,128]{1,0:T(8,128)S(1)}, f32[16,128]{1,0:T(8,128)S(1)}, u32[]{:S(2)}, u32[]{:S(2)}) collective-permute-start(f32[16,128]{1,0:T(8,128)S(1)} %shard_map.68), channel_id=1, source_target_pairs={{0,1},{1,0},{2,3},{3,2},{4,5},{5,4},{6,7},{7,6},{8,9},{9,8},{10,11... | collective-permute-start | bytes 24584 | tf_op jit(solution)/shard_map/ppermute | solution.py:342
  5.1 6.5 %collective-permute-start.2 = (f32[32,128]{1,0:T(8,128)S(1)}, f32[32,128]{1,0:T(8,128)S(1)}, u32[]{:S(2)}, u32[]{:S(2)}) collective-permute-start(f32[32,128]{1,0:T(8,128)S(1)} %pad_maximum_fusion.refs_0_), channel_id=1, source_target_pairs={{2,4},{3,5},{4,2},{5,3},{6,8},{7,9},{8,6},{9,7},{10,12},{11,13},{1... | collective-permute-start | bytes 49160 | tf_op jit(solution)/shard_map/ppermute | solution.py:342
  10.3 1.4 %collective-permute-start.1 = (f32[32,128]{1,0:T(8,128)S(1)}, f32[32,128]{1,0:T(8,128)S(1)}, u32[]{:S(2)}, u32[]{:S(2)}) collective-permute-start(f32[32,128]{1,0:T(8,128)S(1)} %pad_maximum_fusion.refs_0_), channel_id=1, source_target_pairs={{0,2},{1,3},{2,0},{3,1},{4,6},{5,7},{6,4},{7,5},{8,10},{9,11},{10,... | collective-permute-start | bytes 49160 | tf_op jit(solution)/shard_map/ppermute | solution.py:342
